TPU v7x, 32 devices: a whole 2x2x4 slice. The times are simulated.
32 devices in a mesh: rows: 4 (over x, core), slopes: 8 (over z, y).
Axes of the slice: x: 2, y: 2, z: 4, core: 2. Of those that a mesh axis runs over, the one named last changes fastest.
Arguments:
- reconstructor: bfloat16 [5120, 90112], P('rows', 'slopes'), may hold values from -0.375 to 0.375
- cov_slab: bfloat16 [90112, 256], P('slopes', 'rows'), may hold values from -0.4375 to 0.4375
- residual_in: float32 [5120, 5120], P('rows', 'slopes'), may hold values from -6 to 6
- propagation: bfloat16 [5120, 5120], P('rows', 'slopes'), may hold values from -0.078125 to 0.078125
Outputs:
- residual_out: float32 [5120, 5120], P('rows', 'slopes')
- projected: float32 [5120, 5120], P('rows', 'slopes')
All inputs are finite; a program needn't handle non-finite values.
Results may differ from a plain program's by a relative error of at most 0.0046.
Values may be sent and summed in bfloat16 or wider, within the bound.
No kernel may reach another device: no remote copies, remote signals or barrier semaphores. Data moves between devices by JAX's collectives and lax.ppermute only.
A program may use at most 128 MiB of HBM per device.

v0:
```python
import jax
import jax.numpy as jnp
from jax import lax
from jax.sharding import PartitionSpec as P

SLOPES = 90112
SLAB = 256


def spread(x, axis, root):
    mine = lax.axis_index(axis) == root
    return lax.psum(jnp.where(mine, x, jnp.zeros_like(x)), axis)


def body(reconstructor, cov_slab, residual_in, propagation):
    row_index = lax.axis_index("rows")
    slope_index = lax.axis_index("slopes")
    row_block = propagation.shape[0]
    col_block = propagation.shape[1]
    stride = SLOPES // SLAB
    picked_local = reconstructor[:, ::stride]
    d_rows, picked_rows = (
        lax.all_gather(propagation, "slopes", axis=1, tiled=True),
        lax.all_gather(picked_local, "slopes", axis=1, tiled=True),
    )
    partial_sum = jnp.dot(
        reconstructor,
        lax.all_gather(cov_slab, "rows", axis=1, tiled=True),
        preferred_element_type=jnp.float32,
    )
    reach = lax.psum(partial_sum, "slopes").astype(jnp.bfloat16)
    owner = slope_index * col_block // row_block
    offset = jnp.clip(slope_index * col_block - row_index * row_block, 0, row_block - col_block)
    d_local = lax.dynamic_slice_in_dim(d_rows, offset, col_block, 0)
    p_local = lax.dynamic_slice_in_dim(picked_rows, offset, col_block, 0)
    d_block, p_block = (spread(d_local, "rows", owner), spread(p_local, "rows", owner))
    update = lax.dot_general(
        reach, p_block, (((1,), (1,)), ((), ())), preferred_element_type=jnp.float32
    )
    residual_out = residual_in + update
    resid_low = residual_out.astype(jnp.bfloat16)
    columns = d_rows
    front = jnp.dot(
        columns,
        lax.all_gather(resid_low, "rows", axis=0, tiled=True),
        preferred_element_type=jnp.float32,
    ).astype(jnp.bfloat16)
    columns = d_block
    projected = lax.dot_general(
        lax.all_gather(front, "slopes", axis=1, tiled=True),
        columns,
        (((1,), (1,)), ((), ())),
        preferred_element_type=jnp.float32,
    )
    return (residual_out, projected)


def solution(mesh):
    placed = (P("rows", "slopes"), P("slopes", "rows"), P("rows", "slopes"), P("rows", "slopes"))
    return jax.shard_map(
        body,
        mesh=mesh,
        in_specs=placed,
        out_specs=(P("rows", "slopes"), P("rows", "slopes")),
        check_vma=False,
    )
```

profile of v0, /device:TPU:0, one launch (start us, length us, event | category | flops | bytes accessed | tf_op | source)
XLA Modules:
  0.0 648.7 jit_solution(1992956967964907286)
XLA Ops:
  7.2 0.0 all-gather.9.cloned.1.call-start
  7.2 0.7 all-gather.9.cloned.1.call-update
  7.9 0.0 all-gather.5.cloned.1.call-start
  7.9 0.7 all-gather.5.cloned.1.call-update
  8.6 0.0 all-reduce.4.cloned.1.call-start
  8.7 10.7 %slice.3 = bf16[1280,32]{1,0:T(8,128)(2,1)S(1)} slice(bf16[1280,11264]{1,0:T(8,128)(2,1)} %param.4), slice={[0:1280:1], [0:11264:352]} | slice | bytes 163840 | tf_op jit(solution)/shard_map/slice | solution.py:21
  19.5 0.2 copy.7
  19.6 36.3 %all_gather.16 = bf16[1280,256]{0,1:T(8,128)(2,1)S(1)} all-gather(bf16[1280,32]{0,1:T(8,128)(2,1)S(1)} %copy.7), channel_id=1, replica_groups=mesh['rows'=4,'slopes'=8] {'slopes'}, dimensions={1}, use_global_device_ids=true | all-gather | bytes 737280 | tf_op jit(solution)/shard_map/all_gather | solution.py:24
  55.9 0.9 dynamic-slice_select_fusion.1
  56.8 144.5 %all-gather.9.cloned.1.call-done = bf16[1280,5120]{1,0:T(8,128)(2,1)} async-done(((bf16[1280,640]{1,0:T(8,128)(2,1)}), bf16[1280,5120]{1,0:T(8,128)(2,1)}) %all-gather.9.cloned.1.call-update) | async-done | bytes 13107216 | tf_op jit(solution)/shard_map/all_gather | solution.py:23
  201.3 8.0 %dynamic-slice_select_fusion = bf16[640,5120]{1,0:T(8,128)(2,1)} fusion(bf16[1280,5120]{1,0:T(8,128)(2,1)} %all-gather.9.cloned.1.call-done, s32[]{:T(128)S(6)} %min.4, pred[]{:T(512)S(6)} %eq.4), kind=kLoop, calls=%fused_computation | loop fusion | flops 3276800 | bytes 13107205 | tf_op jit(solution)/shard_map/jit(_where)/select_n | solution.py:12
  209.2 0.0 all-reduce.4.cloned.1.call-update
  209.3 0.0 copy-start
  209.3 0.0 all-gather.7.cloned.1.call-start
  209.3 35.1 %all-gather.5.cloned.1.call-done = bf16[11264,256]{0,1:T(8,128)(2,1)} async-done(((bf16[11264,64]{0,1:T(8,128)(2,1)}), bf16[11264,256]{0,1:T(8,128)(2,1)}) %all-gather.5.cloned.1.call-update) | async-done | bytes 5767184 | tf_op jit(solution)/shard_map/all_gather | solution.py:28
  244.4 17.1 %fusion.3 = f32[1280,256]{1,0:T(8,128)} fusion(bf16[1280,11264]{1,0:T(8,128)(2,1)} %param.4, bf16[11264,256]{0,1:T(8,128)(2,1)} %all-gather.5.cloned.1.call-done), kind=kOutput, calls=%fused_computation.7 | convolution fusion | flops 7381975040 | bytes 35913728 | tf_op jit(solution)/shard_map/dot_general | solution.py:26
  261.5 76.8 %all-reduce.5 = bf16[1280,256]{1,0:T(8,128)(2,1)} all-reduce(f32[1280,256]{1,0:T(8,128)} %fusion.3), channel_id=1, replica_groups=mesh['rows'=4,'slopes'=8] {'slopes'}, use_global_device_ids=true, to_apply=%region_0.0 | all-reduce | flops 327680 | bytes 1966080 | tf_op jit(solution)/shard_map/psum | solution.py:31
  338.4 38.3 %all-reduce.4.cloned.1.call-done = (bf16[640,256]{0,1:T(8,128)(2,1)}, bf16[640,5120]{1,0:T(8,128)(2,1)}) async-done(((bf16[640,256]{0,1:T(8,128)(2,1)}, bf16[640,5120]{1,0:T(8,128)(2,1)}), (bf16[640,256]{0,1:T(8,128)(2,1)}, bf16[640,5120]{1,0:T(8,128)(2,1)})) %all-reduce.4.cloned.1.call-update) | async-done | bytes 6881296 | tf_op jit(solution)/shard_map/psum | solution.py:12
  376.7 0.0 copy-done
  376.7 4.1 fusion.2
  380.8 0.0 all-gather.7.cloned.1.call-update
  380.8 0.2 all-gather.11.cloned.1.call-start
  381.0 48.0 %all-gather.7.cloned.1.call-done = bf16[5120,640]{1,0:T(8,128)(2,1)} async-done(((bf16[1280,640]{1,0:T(8,128)(2,1)}), bf16[5120,640]{1,0:T(8,128)(2,1)}) %all-gather.7.cloned.1.call-update) | async-done | bytes 6553616 | tf_op jit(solution)/shard_map/all_gather | solution.py:45
  429.0 14.1 %fusion = bf16[1280,640]{0,1:T(8,128)(2,1)} fusion(bf16[5120,640]{1,0:T(8,128)(2,1)} %all-gather.7.cloned.1.call-done, bf16[1280,5120]{1,0:T(8,128)(2,1)} %all-gather.9.cloned.1.call-done), kind=kOutput, calls=%fused_computation.3 | convolution fusion | flops 8389427200 | bytes 21299200 | tf_op jit(solution)/shard_map/dot_general | solution.py:43
  443.1 0.0 all-gather.11.cloned.1.call-update
  443.1 182.6 %all-gather.11.cloned.1.call-done = bf16[1280,5120]{0,1:T(8,128)(2,1)} async-done(((bf16[1280,640]{0,1:T(8,128)(2,1)}), bf16[1280,5120]{0,1:T(8,128)(2,1)}) %all-gather.11.cloned.1.call-update) | async-done | bytes 13107216 | tf_op jit(solution)/shard_map/all_gather | solution.py:50
  625.8 16.5 %fusion.4 = f32[1280,640]{1,0:T(8,128)} fusion(bf16[1280,5120]{0,1:T(8,128)(2,1)} %all-gather.11.cloned.1.call-done, bf16[640,5120]{1,0:T(8,128)(2,1)} %get-tuple-element.3), kind=kOutput, calls=%fused_computation.8 | convolution fusion | flops 8388608000 | bytes 22937600 | tf_op jit(solution)/shard_map/dot_general | solution.py:49
Async XLA Ops:
  7.2 194.1 %all-gather.9.cloned.1.call-start = ((), (), s32[]{:S(2)}) async-start(), calls=%async_computation.2 | async-start | bytes 14745600 | tf_op jit(solution)/shard_map/all_gather | solution.py:23
  7.9 236.5 %all-gather.5.cloned.1.call-start = ((), (), s32[]{:S(2)}) async-start(), calls=%async_computation | async-start | bytes 7208960 | tf_op jit(solution)/shard_map/all_gather | solution.py:28
  8.6 368.0 %all-reduce.4.cloned.1.call-start = ((), (), s32[]{:S(2)}) async-start(), calls=%async_computation.4 | async-start | bytes 13762560 | tf_op jit(solution)/shard_map/psum | solution.py:12
  209.3 167.4 %copy-start = (f32[1280,640]{1,0:T(8,128)S(1)}, f32[1280,640]{1,0:T(8,128)}, u32[]{:S(2)}) copy-start(f32[1280,640]{1,0:T(8,128)} %param.6) | copy-start | bytes 9830404
  209.3 219.7 %all-gather.7.cloned.1.call-start = ((), (), s32[]{:S(2)}) async-start(), calls=%async_computation.1 | async-start | bytes 8192000 | tf_op jit(solution)/shard_map/all_gather | solution.py:45
  380.8 245.0 %all-gather.11.cloned.1.call-start = ((), (), s32[]{:S(2)}) async-start(), calls=%async_computation.3 | async-start | bytes 14745600 | tf_op jit(solution)/shard_map/all_gather | solution.py:50
Sparse Core Ops, SparseCore 0:
  10.2 191.0 all-gather.8
  202.8 41.5 all-gather.4
  247.4 129.1 all-reduce.3
  380.9 48.0 all-gather.6
  443.2 182.4 all-gather.10
where the time goes:
time: 649 us
  waiting for transfers between devices  450 us (69%)
  blocking collectives  113 us (17%)
  matrix products  51.7 us (8%)
  between operations  13.8 us (2%)
  local copies, waits for them, and re-layouts  10.9 us (2%)
  other arithmetic  8.85 us (1%)
    all_gather x1, waiting for transfers between devices, body(): lax.all_gather(front, 'slopes', axis=1, tiled=True)  183 us
    all_gather x1, waiting for transfers between devices, body(): lax.all_gather(propagation, 'slopes', axis=1, tiled=True)  144 us
    psum x1, blocking collectives, body(): reach = lax.psum(partial_sum, 'slopes').astype(jnp.bfloat16)  76.8 us
    all_gather x1, waiting for transfers between devices, body(): lax.all_gather(resid_low, 'rows', axis=0, tiled=True)  48 us
    psum x1, waiting for transfers between devices, spread(): return lax.psum(jnp.where(mine, x, jnp.zeros_like(x)), axis)  38.3 us
    all_gather x1, blocking collectives, body(): lax.all_gather(picked_local, 'slopes', axis=1, tiled=True)  36.3 us
    all_gather x1, waiting for transfers between devices, body(): lax.all_gather(cov_slab, 'rows', axis=1, tiled=True)  35.1 us
    dot_general x1, matrix products, body(): jnp.dot(reconstructor, lax.all_gather(cov_slab, 'rows', axis=1, tiled=Tru...  17.1 us
  transfers between devices with their start and end apart: 5, of which 5 were waited for; matrix products, arithmetic and copies ran while one was open for 6% of the time, Pallas kernels for 0%

commit v1 on v0

--- a/solution.py
+++ b/solution.py
@@ -1,3 +1,4 @@
+import functools
 import jax
 import jax.numpy as jnp
 from jax import lax
@@ -5,6 +6,16 @@
 
 SLOPES = 90112
 SLAB = 256
+
+
+def map_the_stacks_all(m, chip_axis, on_dim):
+    return jnp.concatenate(
+        lax.all_to_all(jnp.stack(lax.axis_size(chip_axis) * [m], axis=0), chip_axis, 0, 0),
+        axis=on_dim,
+    )
+
+
+corner_enter = functools.partial(map_the_stacks_all, chip_axis="slopes", on_dim=1)
 
 
 def spread(x, axis, root):
@@ -20,7 +31,7 @@
     stride = SLOPES // SLAB
     picked_local = reconstructor[:, ::stride]
     d_rows, picked_rows = (
-        lax.all_gather(propagation, "slopes", axis=1, tiled=True),
+        corner_enter(propagation),
         lax.all_gather(picked_local, "slopes", axis=1, tiled=True),
     )
     partial_sum = jnp.dot(

time: 649 us -> 741 us (1.14)
  blocking collectives: 113 us -> 369 us
  waiting for transfers between devices: 450 us -> 268 us
  local copies, waits for them, and re-layouts: 10.9 us -> 19.5 us
    all_gather x1, blocking collectives: 36.3 us -> 294 us  [body(): lax.all_gather(picked_local, 'slopes', axis=1, tiled=True)]
    all_gather x1 -> x0, waiting for transfers between devices: 144 us -> none  [body(): lax.all_gather(propagation, 'slopes', axis=1, tiled=True)]
    all_gather x1, waiting for transfers between devices: 35.1 us -> 0.02 us  [body(): lax.all_gather(cov_slab, 'rows', axis=1, tiled=True)]
  transfers between devices with their start and end apart: 5 -> 5, of which waited for: 5 -> 3; matrix products, arithmetic and copies ran while one was open for 6% -> 5% of each run, Pallas kernels for 0% -> 0%
where the time goes in v1:
time: 741 us
  blocking collectives  369 us (50%)
  waiting for transfers between devices  268 us (36%)
  matrix products  51.8 us (7%)
  local copies, waits for them, and re-layouts  19.5 us (3%)
  between operations  13.8 us (2%)
  other arithmetic  11.3 us (2%)
  starting transfers between devices  7.65 us (1%)
    all_gather x1, blocking collectives, body(): lax.all_gather(picked_local, 'slopes', axis=1, tiled=True)  294 us
    all_gather x1, waiting for transfers between devices, body(): lax.all_gather(front, 'slopes', axis=1, tiled=True)  183 us
    psum x1, blocking collectives, body(): reach = lax.psum(partial_sum, 'slopes').astype(jnp.bfloat16)  75.1 us
    all_gather x1, waiting for transfers between devices, body(): lax.all_gather(resid_low, 'rows', axis=0, tiled=True)  48 us
    psum x1, waiting for transfers between devices, spread(): return lax.psum(jnp.where(mine, x, jnp.zeros_like(x)), axis)  36.5 us
    dot_general x1, matrix products, body(): jnp.dot(reconstructor, lax.all_gather(cov_slab, 'rows', axis=1, tiled=Tru...  17 us
    dot_general x1, matrix products, body(): lax.dot_general(lax.all_gather(front, 'slopes', axis=1, tiled=True), colu...  16.5 us
  transfers between devices with their start and end apart: 5, of which 3 were waited for; matrix products, arithmetic and copies ran while one was open for 5% of the time, Pallas kernels for 0%

profile of v1, /device:TPU:0, one launch (start us, length us, event | category | flops | bytes accessed | tf_op | source)
XLA Modules:
  0.0 740.8 jit_solution(12986507380801744064)
XLA Ops:
  7.2 2.7 copy.8
  9.9 5.6 stack.2
  15.5 7.3 all-to-all-start
  22.8 0.0 all-gather.4.cloned.1.call-start
  22.8 0.7 all-gather.4.cloned.1.call-update
  23.5 0.0 all-reduce.4.cloned.1.call-start
  23.6 11.1 %slice.3 = bf16[1280,32]{1,0:T(8,128)(2,1)S(1)} slice(bf16[1280,11264]{1,0:T(8,128)(2,1)} %param.4), slice={[0:1280:1], [0:11264:352]} | slice | bytes 163840 | tf_op jit(solution)/shard_map/slice | solution.py:32
  34.7 0.2 copy.9
  34.8 293.7 %all_gather.13 = bf16[1280,256]{0,1:T(8,128)(2,1)S(1)} all-gather(bf16[1280,32]{0,1:T(8,128)(2,1)S(1)} %copy.9), channel_id=1, replica_groups=mesh['rows'=4,'slopes'=8] {'slopes'}, dimensions={1}, use_global_device_ids=true | all-gather | bytes 737280 | tf_op jit(solution)/shard_map/all_gather | solution.py:35
  328.5 0.9 dynamic-slice_select_fusion.1
  329.4 0.0 all-to-all-done
  329.4 10.4 %dynamic-slice_select_fusion = bf16[640,5120]{0,1:T(8,128)(2,1)} fusion(bf16[1280,5120]{0,1:T(8,128)(2,1)} %bitcast.1, s32[]{:T(128)S(6)} %min.4, pred[]{:T(512)S(6)} %eq.4), kind=kLoop, calls=%fused_computation | loop fusion | flops 3276800 | bytes 13107205 | tf_op jit(solution)/shard_map/jit(_where)/select_n | solution.py:23
  339.8 0.0 all-reduce.4.cloned.1.call-update
  339.9 0.0 copy-start
  339.9 0.0 all-gather.6.cloned.1.call-start
  339.9 0.0 all-gather.4.cloned.1.call-done
  340.0 17.0 %fusion.3 = f32[1280,256]{1,0:T(8,128)} fusion(bf16[1280,11264]{1,0:T(8,128)(2,1)} %param.4, bf16[11264,256]{0,1:T(8,128)(2,1)} %all-gather.4.cloned.1.call-done), kind=kOutput, calls=%fused_computation.7 | convolution fusion | flops 7381975040 | bytes 35913728 | tf_op jit(solution)/shard_map/dot_general | solution.py:37
  357.0 75.1 %all-reduce.5 = bf16[1280,256]{1,0:T(8,128)(2,1)} all-reduce(f32[1280,256]{1,0:T(8,128)} %fusion.3), channel_id=1, replica_groups=mesh['rows'=4,'slopes'=8] {'slopes'}, use_global_device_ids=true, to_apply=%region_0.0 | all-reduce | flops 327680 | bytes 1966080 | tf_op jit(solution)/shard_map/psum | solution.py:42
  432.1 36.5 %all-reduce.4.cloned.1.call-done = (bf16[640,256]{0,1:T(8,128)(2,1)}, bf16[640,5120]{0,1:T(8,128)(2,1)}) async-done(((bf16[640,256]{0,1:T(8,128)(2,1)}, bf16[640,5120]{0,1:T(8,128)(2,1)}), (bf16[640,256]{0,1:T(8,128)(2,1)}, bf16[640,5120]{0,1:T(8,128)(2,1)})) %all-reduce.4.cloned.1.call-update) | async-done | bytes 6881296 | tf_op jit(solution)/shard_map/psum | solution.py:23
  468.5 0.0 copy-done
  468.5 4.1 fusion.2
  472.6 0.0 all-gather.6.cloned.1.call-update
  472.7 0.2 all-gather.8.cloned.1.call-start
  472.9 48.0 %all-gather.6.cloned.1.call-done = bf16[5120,640]{1,0:T(8,128)(2,1)} async-done(((bf16[1280,640]{1,0:T(8,128)(2,1)}), bf16[5120,640]{1,0:T(8,128)(2,1)}) %all-gather.6.cloned.1.call-update) | async-done | bytes 6553616 | tf_op jit(solution)/shard_map/all_gather | solution.py:56
  520.9 14.2 %fusion = bf16[1280,640]{0,1:T(8,128)(2,1)} fusion(bf16[5120,640]{1,0:T(8,128)(2,1)} %all-gather.6.cloned.1.call-done, bf16[1280,5120]{0,1:T(8,128)(2,1)} %bitcast.1), kind=kOutput, calls=%fused_computation.3 | convolution fusion | flops 8389427200 | bytes 21299200 | tf_op jit(solution)/shard_map/dot_general | solution.py:54
  535.1 0.0 all-gather.8.cloned.1.call-update
  535.1 182.6 %all-gather.8.cloned.1.call-done = bf16[1280,5120]{0,1:T(8,128)(2,1)} async-done(((bf16[1280,640]{0,1:T(8,128)(2,1)}), bf16[1280,5120]{0,1:T(8,128)(2,1)}) %all-gather.8.cloned.1.call-update) | async-done | bytes 13107216 | tf_op jit(solution)/shard_map/all_gather | solution.py:61
  717.7 16.5 %fusion.4 = f32[1280,640]{1,0:T(8,128)} fusion(bf16[1280,5120]{0,1:T(8,128)(2,1)} %all-gather.8.cloned.1.call-done, bf16[640,5120]{0,1:T(8,128)(2,1)} %get-tuple-element.3), kind=kOutput, calls=%fused_computation.8 | convolution fusion | flops 8388608000 | bytes 22937600 | tf_op jit(solution)/shard_map/dot_general | solution.py:60
Async XLA Ops:
  15.5 314.0 %all-to-all-start = ((bf16[8,1280,640]{1,2,0:T(8,128)(2,1)}), bf16[8,1280,640]{1,2,0:T(8,128)(2,1)}, u32[]{:S(2)}, u32[]{:S(2)}) async-start(bf16[8,1280,640]{1,2,0:T(8,128)(2,1)} %stack.2), calls=%async_computation | async-start | bytes 26214400 | tf_op jit(solution)/shard_map/all_to_all | solution.py:13
  22.8 317.2 %all-gather.4.cloned.1.call-start = ((), (), s32[]{:S(2)}) async-start(), calls=%async_computation.1 | async-start | bytes 7208960 | tf_op jit(solution)/shard_map/all_gather | solution.py:39
  23.5 445.0 %all-reduce.4.cloned.1.call-start = ((), (), s32[]{:S(2)}) async-start(), calls=%async_computation.4 | async-start | bytes 13762560 | tf_op jit(solution)/shard_map/psum | solution.py:23
  339.9 128.7 %copy-start = (f32[1280,640]{1,0:T(8,128)S(1)}, f32[1280,640]{1,0:T(8,128)}, u32[]{:S(2)}) copy-start(f32[1280,640]{1,0:T(8,128)} %param.6) | copy-start | bytes 9830404
  339.9 181.0 %all-gather.6.cloned.1.call-start = ((), (), s32[]{:S(2)}) async-start(), calls=%async_computation.2 | async-start | bytes 8192000 | tf_op jit(solution)/shard_map/all_gather | solution.py:56
  472.7 245.1 %all-gather.8.cloned.1.call-start = ((), (), s32[]{:S(2)}) async-start(), calls=%async_computation.3 | async-start | bytes 14745600 | tf_op jit(solution)/shard_map/all_gather | solution.py:61
Sparse Core Ops, SparseCore 0:
  25.1 44.7 all-gather.3
  340.0 128.5 all-reduce.3
  472.8 48.0 all-gather.5
  535.2 182.4 all-gather.7
